TPU v7x, 256 devices: a whole 4x4x8 slice. The times are simulated.
256 devices in a mesh: inline: 32 (over z, y_lo, core), shot: 8 (over y_hi, x).
Axes of the slice: x: 4, y: 4 (y_hi: 2, y_lo: 2; y = y_hi * 2 + y_lo), z: 8, core: 2. Of those that a mesh axis runs over, the one named last changes fastest.
Arguments:
- source: bfloat16 [32, 1024, 32, 256], P('shot', 'inline'), may hold values from -6 to 6
- receiver: bfloat16 [32, 1024, 32, 256], P('shot', 'inline'), may hold values from -6 to 6
Outputs:
- offset_image: float32 [129, 1024, 256], P(None, 'inline', 'shot')
All inputs are finite; a program needn't handle non-finite values.
Results may differ from a plain program's by a relative error of at most 0.0003.
Values may be sent and summed in bfloat16 or wider, within the bound.
A program may use at most 192 MiB of HBM per device.

v0:
```python
import jax
import jax.numpy as jnp
from jax import lax
from jax.sharding import PartitionSpec as P


def shifted(value, axis, steps):
    count = lax.axis_size(axis)
    initial, last = (max(0, -steps), min(count, count - steps))
    return lax.ppermute(value, axis, [(source, source + steps) for source in range(initial, last)])


def band_rows(product, width, lags):
    rows = product.shape[0]
    cross = product.shape[2]
    flat = product.reshape(rows * width, cross)
    flat = jnp.pad(flat, ((0, rows), (0, 0)))
    skewed = flat.reshape(rows, width + 1, cross)[:, :lags, :]
    return jnp.transpose(skewed, (1, 0, 2))


def direct_shift(slab, offset):
    return shifted(slab, "inline", offset)


def extend(receiver):
    near_left = direct_shift(receiver, 1)
    far_left = direct_shift(receiver, 2)
    near_right = direct_shift(receiver, -1)
    far_right = direct_shift(receiver, -2)
    return jnp.concatenate((far_left, near_left, receiver, near_right, far_right), axis=1)


def correlate(source, receiver):
    cells = source.shape[1]
    lag_half = 2 * cells
    extended = extend(receiver)
    width = cells + 2 * lag_half
    product = jnp.einsum("sity,szty->izy", source, extended, preferred_element_type=jnp.float32)
    return band_rows(product, width, 2 * lag_half + 1)


def on_device(source, receiver):
    times = source.shape[2]
    all_shots = source.shape[0] * lax.axis_size("shot")
    partial_image = correlate(source, receiver)
    summed = lax.psum_scatter(partial_image, "shot", scatter_dimension=2, tiled=True)
    return summed * (1.0 / (times * all_shots) ** 0.5)


def solution(mesh):
    placed = (P("shot", "inline", None, None), P("shot", "inline", None, None))
    return jax.shard_map(
        on_device, mesh=mesh, in_specs=placed, out_specs=P(None, "inline", "shot"), check_vma=False
    )
```

profile of v0, /device:TPU:1, one launch (start us, length us, event | category | flops | bytes accessed | tf_op | source)
XLA Modules:
  0.0 416.1 jit_solution(14737564646017602555)
XLA Ops:
  6.5 0.0 copy-start
  6.5 0.0 reduce-scatter.2.cloned.1.call-start
  6.5 5.5 %collective-permute-start = (bf16[4,32,32,256]{3,2,1,0:T(8,128)(2,1)}, bf16[4,32,32,256]{3,2,1,0:T(8,128)(2,1)}, u32[]{:S(2)}, u32[]{:S(2)}) collective-permute-start(bf16[4,32,32,256]{3,2,1,0:T(8,128)(2,1)} %param.3), channel_id=1, source_target_pairs={{0,16},{8,24},{16,32},{24,40},{32,48},{40,56},{48,64},{56,72},{64,... | collective-permute-start | bytes 6291464 | tf_op jit(solution)/shard_map/ppermute | solution.py:10
  12.0 2.9 collective-permute-start.1
  15.0 2.7 collective-permute-start.2
  17.7 1.3 collective-permute-start.3
  19.0 15.2 %copy.19 = bf16[4,32,32,256]{1,2,0,3:T(8,128)(2,1)} copy(bf16[4,32,32,256]{3,2,1,0:T(8,128)(2,1)} %param.3) | data formatting | bytes 4194304 | tf_op args[1]
  34.2 0.0 copy-done
  34.2 12.0 %copy.22 = bf16[4,32,32,256]{2,1,0,3:T(8,128)(2,1)} copy(bf16[4,32,32,256]{3,2,1,0:T(8,128)(2,1)S(1)} %copy-done) | data formatting | bytes 4194304 | tf_op args[0]
  46.2 76.6 %collective-permute-done = bf16[4,32,32,256]{3,2,1,0:T(8,128)(2,1)} collective-permute-done((bf16[4,32,32,256]{3,2,1,0:T(8,128)(2,1)}, bf16[4,32,32,256]{3,2,1,0:T(8,128)(2,1)}, u32[]{:S(2)}, u32[]{:S(2)}) %collective-permute-start) | collective-permute-done | bytes 2097184 | tf_op jit(solution)/shard_map/ppermute | solution.py:10
  122.7 15.2 %copy.17 = bf16[4,32,32,256]{1,2,0,3:T(8,128)(2,1)} copy(bf16[4,32,32,256]{3,2,1,0:T(8,128)(2,1)} %collective-permute-done) | data formatting | bytes 4194304 | tf_op jit(solution)/shard_map/ppermute | solution.py:10
  137.9 8.4 %collective-permute-done.1 = bf16[4,32,32,256]{3,2,1,0:T(8,128)(2,1)} collective-permute-done((bf16[4,32,32,256]{3,2,1,0:T(8,128)(2,1)}, bf16[4,32,32,256]{3,2,1,0:T(8,128)(2,1)}, u32[]{:S(2)}, u32[]{:S(2)}) %collective-permute-start.1) | collective-permute-done | bytes 2097184 | tf_op jit(solution)/shard_map/ppermute | solution.py:10
  146.3 15.2 %copy.18 = bf16[4,32,32,256]{1,2,0,3:T(8,128)(2,1)} copy(bf16[4,32,32,256]{3,2,1,0:T(8,128)(2,1)} %collective-permute-done.1) | data formatting | bytes 4194304 | tf_op jit(solution)/shard_map/ppermute | solution.py:10
  161.5 0.0 collective-permute-done.2
  161.5 15.2 %copy.20 = bf16[4,32,32,256]{1,2,0,3:T(8,128)(2,1)} copy(bf16[4,32,32,256]{3,2,1,0:T(8,128)(2,1)} %collective-permute-done.2) | data formatting | bytes 4194304 | tf_op jit(solution)/shard_map/ppermute | solution.py:10
  176.8 0.0 collective-permute-done.3
  176.8 15.3 %copy.21 = bf16[4,32,32,256]{1,2,0,3:T(8,128)(2,1)} copy(bf16[4,32,32,256]{3,2,1,0:T(8,128)(2,1)} %collective-permute-done.3) | data formatting | bytes 4194304 | tf_op jit(solution)/shard_map/ppermute | solution.py:10
  192.0 44.4 %concatenate.3 = bf16[4,160,32,256]{1,2,0,3:T(8,128)(2,1)} concatenate(bf16[4,32,32,256]{1,2,0,3:T(8,128)(2,1)} %copy.17, bf16[4,32,32,256]{1,2,0,3:T(8,128)(2,1)} %copy.18, bf16[4,32,32,256]{1,2,0,3:T(8,128)(2,1)} %copy.19, bf16[4,32,32,256]{1,2,0,3:T(8,128)(2,1)} %copy.20, bf16[4,32,32,256]{1,2,0,3:T(8,128)(2,1)} %copy.21), dimensions={1} | concatenate | bytes 20971520 | tf_op jit(solution)/shard_map/concatenate | solution.py:31
  236.4 14.3 %convolution_bitcast_fusion = f32[32,160,256]{1,0,2:T(8,128)} fusion(bf16[4,32,32,256]{2,1,0,3:T(8,128)(2,1)} %copy.22, bf16[4,160,32,256]{1,2,0,3:T(8,128)(2,1)} %concatenate.3), kind=kOutput, calls=%fused_computation.1 | convolution fusion | flops 335544320 | bytes 17825792 | tf_op jit(solution)/shard_map/sity,szty->izy/dot_general | solution.py:39
  250.7 9.1 %copy.23 = f32[32,160,256]{2,1,0:T(8,128)} copy(f32[32,160,256]{1,0,2:T(8,128)} %convolution_bitcast_fusion) | data formatting | bytes 10485760 | tf_op jit(solution)/shard_map/sity,szty->izy/transpose | solution.py:39
  259.8 5.2 %pad.4 = f32[5152,256]{1,0:T(8,128)} pad(f32[5120,256]{1,0:T(8,128)} %bitcast.10, f32[]{:T(128)} %constant.1.clone.1), padding=0_32x0_0 | pad | bytes 10518532 | tf_op jit(solution)/shard_map/jit(_pad)/pad | solution.py:17
  265.0 5.6 %reshape.7 = f32[32,161,256]{2,1,0:T(8,128)} reshape(f32[5152,256]{1,0:T(8,128)} %pad.4) | data formatting | bytes 10551296 | tf_op jit(solution)/shard_map/reshape | solution.py:18
  270.6 4.6 %slice_bitcast_fusion = f32[129,32,256]{2,0,1:T(8,128)} fusion(f32[32,161,256]{2,1,0:T(8,128)} %reshape.7), kind=kLoop, calls=%fused_computation | loop fusion | bytes 8454144 | tf_op jit(solution)/shard_map/transpose | solution.py:19
  275.2 8.8 %copy.24 = f32[129,32,256]{0,1,2:T(8,128)} copy(f32[129,32,256]{2,0,1:T(8,128)} %slice_bitcast_fusion) | data formatting | bytes 8454144 | tf_op jit(solution)/shard_map/transpose | solution.py:19
  284.0 0.0 reduce-scatter.2.cloned.1.call-update
  284.0 122.4 %reduce-scatter.2.cloned.1.call-done = f32[129,32,32]{0,1,2:T(8,128)} async-done(((f32[129,32,256]{0,1,2:T(8,128)}), f32[129,32,32]{0,1,2:T(8,128)}) %reduce-scatter.2.cloned.1.call-update) | async-done | bytes 528400 | tf_op jit(solution)/shard_map/reduce_scatter | solution.py:47
  406.4 1.3 broadcast_multiply_fusion
  407.7 1.6 copy.25
Async XLA Ops:
  6.5 27.7 %copy-start = (bf16[4,32,32,256]{3,2,1,0:T(8,128)(2,1)S(1)}, bf16[4,32,32,256]{3,2,1,0:T(8,128)(2,1)}, u32[]{:S(2)}) copy-start(bf16[4,32,32,256]{3,2,1,0:T(8,128)(2,1)} %param.2) | copy-start | bytes 6291460
  6.5 399.8 %reduce-scatter.2.cloned.1.call-start = ((), (), s32[]{:S(2)}) async-start(), calls=%async_computation.1 | async-start | bytes 9437184 | tf_op jit(solution)/shard_map/reduce_scatter | solution.py:47
  6.5 116.2 %collective-permute-start = (bf16[4,32,32,256]{3,2,1,0:T(8,128)(2,1)}, bf16[4,32,32,256]{3,2,1,0:T(8,128)(2,1)}, u32[]{:S(2)}, u32[]{:S(2)}) collective-permute-start(bf16[4,32,32,256]{3,2,1,0:T(8,128)(2,1)} %param.3), channel_id=1, source_target_pairs={{0,16},{8,24},{16,32},{24,40},{32,48},{40,56},{48,64},{56,72},{64,... | collective-permute-start | bytes 6291464 | tf_op jit(solution)/shard_map/ppermute | solution.py:10
  12.0 134.3 %collective-permute-start.1 = (bf16[4,32,32,256]{3,2,1,0:T(8,128)(2,1)}, bf16[4,32,32,256]{3,2,1,0:T(8,128)(2,1)}, u32[]{:S(2)}, u32[]{:S(2)}) collective-permute-start(bf16[4,32,32,256]{3,2,1,0:T(8,128)(2,1)} %param.3), channel_id=1, source_target_pairs={{0,8},{8,16},{16,24},{24,32},{32,40},{40,48},{48,56},{56,64},{64,7... | collective-permute-start | bytes 6291464 | tf_op jit(solution)/shard_map/ppermute | solution.py:10
  15.0 146.6 %collective-permute-start.2 = (bf16[4,32,32,256]{3,2,1,0:T(8,128)(2,1)}, bf16[4,32,32,256]{3,2,1,0:T(8,128)(2,1)}, u32[]{:S(2)}, u32[]{:S(2)}) collective-permute-start(bf16[4,32,32,256]{3,2,1,0:T(8,128)(2,1)} %param.3), channel_id=1, source_target_pairs={{8,0},{16,8},{24,16},{32,24},{40,32},{48,40},{56,48},{64,56},{72,6... | collective-permute-start | bytes 6291464 | tf_op jit(solution)/shard_map/ppermute | solution.py:10
  17.7 159.1 %collective-permute-start.3 = (bf16[4,32,32,256]{3,2,1,0:T(8,128)(2,1)}, bf16[4,32,32,256]{3,2,1,0:T(8,128)(2,1)}, u32[]{:S(2)}, u32[]{:S(2)}) collective-permute-start(bf16[4,32,32,256]{3,2,1,0:T(8,128)(2,1)} %param.3), channel_id=1, source_target_pairs={{16,0},{24,8},{32,16},{40,24},{48,32},{56,40},{64,48},{72,56},{80,... | collective-permute-start | bytes 6291464 | tf_op jit(solution)/shard_map/ppermute | solution.py:10
Sparse Core Ops, SparseCore 0:
  284.1 122.1 reduce-scatter.1
where the time goes:
time: 418 us; the launch traced here: 416 us
  waiting for transfers between devices  207 us (50%)
  local copies, waits for them, and re-layouts  167 us (40%)
  matrix products  14.3 us (3%)
  between operations  13.4 us (3%)
  starting transfers between devices  12.4 us (3%)
    reduce_scatter x1, waiting for transfers between devices, on_device(): lax.psum_scatter(partial_image, 'shot', scatter_dimension=2, tiled=True)  122 us
    ppermute x4, waiting for transfers between devices, shifted(): lax.ppermute(value, axis, [(source, source + steps) for source in range(i...  85 us
    ppermute x4, local copies, waits for them, and re-layouts, shifted(): lax.ppermute(value, axis, [(source, source + steps) for source in range(i...  60.9 us
    concatenate x1, local copies, waits for them, and re-layouts, extend(): jnp.concatenate((far_left, near_left, receiver, near_right, far_right), a...  44.4 us
    unnamed x4, local copies, waits for them, and re-layouts  27.2 us
    dot_general x1, matrix products, correlate(): jnp.einsum('sity,szty->izy', source, extended, preferred_element_type=jnp...  14.3 us
    transpose x2, local copies, waits for them, and re-layouts, band_rows(): return jnp.transpose(skewed, (1, 0, 2))  13.4 us
    ppermute x4, starting transfers between devices, shifted(): lax.ppermute(value, axis, [(source, source + steps) for source in range(i...  12.4 us
  transfers between devices with their start and end apart: 5, of which 3 were waited for; matrix products, arithmetic and copies ran while one was open for 18% of the time, Pallas kernels for 0%

commit v1 on v0

v1 whole, which is shorter than its diff:
```python
import functools

import jax
import jax.numpy as jnp
from jax import lax
from jax.experimental import pallas as pl
from jax.experimental.pallas import tpu as pltpu
from jax.sharding import PartitionSpec as P

MESH = pl.DeviceIdType.MESH
F32 = jnp.float32
BF16 = jnp.bfloat16
LANES = 128
RINGS = 4
HOPS = (2, 1, 3, 0)
STEPS = [(part, hop) for part in range(2) for hop in HOPS]
FAR_UP, FAR_DOWN, SUM_UP, SUM_DOWN, NEAR_UP, NEAR_DOWN = range(6)


def kernel(
    source, receiver, out,
    raw, turned, left, right, partial, inbox, across,
    raw_sem, halo_send, halo_recv, ring_send, ring_recv, across_send, across_recv,
):
    shots, cells, times, _ = source.shape
    block = left.shape[0] // 8
    half = block // 2
    owners = lax.axis_size("inline")
    me, shot = lax.axis_index("inline"), lax.axis_index("shot")
    core, low, x, high = me % 2, (me // 2) % 2, shot % RINGS, shot // RINGS
    core_mate = me + 1 - 2 * core
    low_mate = me + 2 - 4 * low
    along = (me + 4 - 8 * low + owners) % owners
    against = (me - 4 + 8 * low + owners) % owners
    up = high * RINGS + (x + 1) % RINGS
    down = high * RINGS + (x + RINGS - 1) % RINGS
    high_mate = (1 - high) * RINGS + x
    peers = [(core_mate, shot), (low_mate, shot), (along, shot), (against, shot), (me, up), (me, down), (me, high_mate)]

    def place(inline, line):
        return {"inline": inline, "shot": line}

    def tile(part):
        return pl.multiple_of(((high + 1 + part) % 2) * LANES, LANES)

    def first(step):
        part, hop = STEPS[step]
        return tile(part) + ((x + hop) % RINGS) * block

    loads = []
    for part in range(2):
        for which, array in enumerate((receiver, source)):
            loads.append(
                pltpu.make_async_copy(
                    array.at[:, :, :, pl.ds(tile(part), LANES)], raw.at[part, which], raw_sem.at[part, which]
                )
            )
            loads[-1].start()

    barrier = pltpu.get_barrier_semaphore()
    for inline, line in peers:
        pl.semaphore_signal(barrier, inc=1, device_id=place(inline, line), device_id_type=MESH)

    def relayout(part, which):
        loads[2 * part + which].wait()

        def turn(i, carry):
            rows = jnp.concatenate([raw[part, which, s, i].astype(F32) for s in range(shots)], axis=0)
            row = cells - 1 - i if which else i
            turned[pl.ds(pl.multiple_of(row * LANES, LANES), LANES), :] = rows.T
            return carry

        def gather(y, carry):
            value = turned[pl.ds(y, cells, stride=LANES), :].astype(BF16)
            if which:
                left[tile(part) + y] = value
            else:
                right[2, tile(part) + y] = value
            return carry

        lax.fori_loop(0, cells, turn, 0, unroll=2)
        lax.fori_loop(0, LANES, gather, 0, unroll=8)

    def halo(kind, step, slot, target_slot, inline):
        rows = pl.ds(first(step), block)
        return pltpu.make_async_remote_copy(
            src_ref=right.at[slot, rows],
            dst_ref=right.at[target_slot, rows],
            send_sem=halo_send.at[kind, step],
            recv_sem=halo_recv.at[kind, step],
            device_id=place(inline, shot),
            device_id_type=MESH,
        )

    def own_core(step):
        return halo(0, step, 2, 1 + 2 * core, core_mate)

    def own_low(step):
        return halo(1, step, 2, 4 * low, low_mate)

    def relay_along(step):
        return halo(2, step, 4 * (1 - low), 4 * low, along)

    def relay_core(step):
        return halo(3, step, 4 * (1 - core), 3 - 2 * core, core_mate)

    def ring(kind, part, step, which, line):
        return pltpu.make_async_remote_copy(
            src_ref=partial.at[step, which],
            dst_ref=inbox.at[part, kind],
            send_sem=ring_send.at[part, kind],
            recv_sem=ring_recv.at[part, kind],
            device_id=place(me, line),
            device_id_type=MESH,
        )

    lane = lax.broadcasted_iota(jnp.int32, (cells, LANES), 1)
    row = lax.broadcasted_iota(jnp.int32, (cells, LANES), 0)
    inside = (lane >= cells * (2 - me)) & (lane < cells * (owners + 2 - me))
    beyond = lane < cells * (owners + 2 - me) - LANES
    straight = lane < LANES - cells + 1 + row

    def correlate(step, which, added=None):
        start = first(step) + which * half

        def one(m, edge):
            y = start + m
            s = left[y]
            near = jnp.concatenate([right[slot, y] for slot in range(4)], axis=0)
            contract = (((1,), (1,)), ((), ()))
            a = lax.dot_general(s, near, contract, preferred_element_type=F32)
            b = lax.dot_general(s, right[4, y], contract, preferred_element_type=F32)
            b = jnp.concatenate([b, jnp.zeros((cells, LANES - cells), F32)], axis=1)
            a = jnp.where(inside, a, 0.0)
            b = jnp.where(beyond, b, 0.0)
            a = pltpu.roll(a, LANES - cells + 1, axis=1, stride=1, stride_axis=0)
            b = pltpu.roll(b, LANES - cells + 1, axis=1, stride=1, stride_axis=0)
            band = jnp.where(straight, a, b)
            if added is not None:
                band = band + added[m]
            partial[step, which, m] = band
            return jnp.where(lane == m, pltpu.roll(b, m, axis=1), edge)

        edge = lax.fori_loop(0, half, one, jnp.zeros((cells, LANES), F32), unroll=4)
        if added is not None:
            edge = edge + added[half]
        partial[step, which, half] = edge

    sent = []

    def go(copy):
        copy.start()
        sent.append(copy)
        return copy

    def process(step):
        own_core(step).wait_recv()
        relay_core(step).wait_recv()
        part, hop = STEPS[step]
        if hop == 2:
            correlate(step, 0)
            go(ring(FAR_UP, part, step, 0, up))
            correlate(step, 1)
            go(ring(FAR_DOWN, part, step, 1, down))
        elif hop == 1:
            correlate(step, 1)
            go(ring(NEAR_UP, part, step, 1, up))
            ring(FAR_UP, part, step, 0, up).wait_recv()
            correlate(step, 0, inbox.at[part, FAR_UP])
            go(ring(SUM_UP, part, step, 0, up))
        elif hop == 3:
            correlate(step, 0)
            go(ring(NEAR_DOWN, part, step, 0, down))
            ring(FAR_DOWN, part, step, 1, down).wait_recv()
            correlate(step, 1, inbox.at[part, FAR_DOWN])
            go(ring(SUM_DOWN, part, step, 1, down))
        else:
            correlate(step, 0)
            correlate(step, 1)

    def gather_ring(part):
        step = STEPS.index((part, 0))
        for kind, which in ((SUM_UP, 0), (NEAR_DOWN, 0), (SUM_DOWN, 1), (NEAR_UP, 1)):
            ring(kind, part, step, which, up).wait_recv()

        def add(m, carry):
            for which, kinds in enumerate(((SUM_UP, NEAR_DOWN), (SUM_DOWN, NEAR_UP))):
                total = partial[step, which, m] + inbox[part, kinds[0], m] + inbox[part, kinds[1], m]
                if part:
                    total = total + across[which, m]
                partial[step, which, m] = total
            return carry

        if part:
            exchange().wait_recv()
        lax.fori_loop(0, half + 1, add, 0)

    def exchange():
        return pltpu.make_async_remote_copy(
            src_ref=partial.at[STEPS.index((0, 0))],
            dst_ref=across,
            send_sem=across_send,
            recv_sem=across_recv,
            device_id=place(me, high_mate),
            device_id_type=MESH,
        )

    relayout(0, 0)
    pl.semaphore_wait(barrier, len(peers))
    for step in range(4):
        go(own_low(step))
        go(own_core(step))
    relayout(0, 1)
    relayout(1, 0)
    for step in range(4, 8):
        go(own_low(step))
        go(own_core(step))

    def forward(step):
        own_low(step).wait_recv()
        go(relay_along(step))

    def share(step):
        relay_along(step).wait_recv()
        go(relay_core(step))

    forward(0)
    relayout(1, 1)
    forward(1)
    share(0)
    for step in range(8):
        if step + 2 < 8:
            forward(step + 2)
        if step + 1 < 8:
            share(step + 1)
        process(step)
        if step == 4:
            gather_ring(0)
            go(exchange())
    gather_ring(1)

    last = STEPS.index((1, 0))
    total = partial.at[last]
    for which in range(2):
        edge = total[which, half].T
        rows = pl.ds(which * half, half)
        for i in range(cells):
            back = cells - 1 - i
            out[i, rows, 0:LANES] = total[which, 0:half, back, :]
            out[i, rows, LANES : LANES + 1] = edge[0:half, back : back + 1]
    for copy in sent:
        copy.wait_send()


def on_device(source, receiver):
    shots, cells, times, cross = source.shape
    all_shots = shots * lax.axis_size("shot")
    block = cross // 8
    half = block // 2
    scale = 1.0 / (times * all_shots) ** 0.5
    lags = 4 * cells + 1
    image = pl.pallas_call(
        kernel,
        out_shape=jax.ShapeDtypeStruct((cells, block, lags), F32),
        in_specs=[pl.BlockSpec(memory_space=pl.ANY)] * 2,
        out_specs=pl.BlockSpec(memory_space=pltpu.VMEM),
        scratch_shapes=[
            pltpu.VMEM((2, 2, shots, cells, times, LANES), BF16),
            pltpu.VMEM((cells * LANES, LANES), F32),
            pltpu.VMEM((cross, cells, LANES), BF16),
            pltpu.VMEM((5, cross, cells, LANES), BF16),
            pltpu.VMEM((8, 2, half + 1, cells, LANES), F32),
            pltpu.VMEM((2, 6, half + 1, cells, LANES), F32),
            pltpu.VMEM((2, half + 1, cells, LANES), F32),
            pltpu.SemaphoreType.DMA((2, 2)),
            pltpu.SemaphoreType.DMA((4, 8)),
            pltpu.SemaphoreType.DMA((4, 8)),
            pltpu.SemaphoreType.DMA((2, 6)),
            pltpu.SemaphoreType.DMA((2, 6)),
            pltpu.SemaphoreType.DMA,
            pltpu.SemaphoreType.DMA,
        ],
        compiler_params=pltpu.CompilerParams(collective_id=0, has_side_effects=True, vmem_limit_bytes=60 * 2**20),
    )(source, receiver)
    return jnp.transpose(image * scale, (2, 0, 1))


def solution(mesh):
    placed = (P("shot", "inline", None, None), P("shot", "inline", None, None))
    return jax.shard_map(
        on_device, mesh=mesh, in_specs=placed, out_specs=P(None, "inline", "shot"), check_vma=False
    )
```

time: 418 us -> 81.4 us (0.19)
  the two profiles are of different devices: /device:TPU:1 before, /device:TPU:2 now
where the time goes in v1:
time: 81.4 us; the launch traced here: 81.3 us
  Pallas kernels  79 us (97%)
  other arithmetic  2.31 us (3%)
    pallas_call x1, Pallas kernels, on_device(): pl.pallas_call(kernel, out_shape=jax.ShapeDtypeStruct((cells, block, lags...  79 us
    transpose x1, other arithmetic, on_device(): return jnp.transpose(image * scale, (2, 0, 1))  2.31 us

profile of v1, /device:TPU:2, one launch (start us, length us, event | category | flops | bytes accessed | tf_op | source)
XLA Modules:
  0.0 81.3 jit_solution(6542072229588166945)
XLA Ops:
  0.0 79.0 %shard_map.28 = f32[32,32,129]{2,1,0:T(8,128)} custom-call(bf16[4,32,32,256]{3,2,1,0:T(8,128)(2,1)} %source.1, bf16[4,32,32,256]{3,2,1,0:T(8,128)(2,1)} %receiver.1), custom_call_target="tpu_custom_call" | custom-call | tf_op jit(solution)/shard_map/pallas_call | solution.py:262
  79.0 2.3 %multiply_bitcast_fusion = f32[129,32,32]{0,2,1:T(8,128)} fusion(f32[32,32,129]{2,1,0:T(8,128)} %shard_map.28), kind=kLoop, calls=%fused_computation | loop fusion | flops 132096 | bytes 1056768 | tf_op jit(solution)/shard_map/transpose | solution.py:285

commit v2 on v0

v2 whole, which is shorter than its diff:
```python
import jax
import jax.numpy as jnp
from jax import lax
from jax.experimental import pallas as pl
from jax.experimental.pallas import tpu as pltpu
from jax.sharding import PartitionSpec as P

MESH = pl.DeviceIdType.MESH
F32 = jnp.float32
BF16 = jnp.bfloat16
LANES = 128
SUBLANES = 8
RINGS = 4
QUAD = 4
SIZES = (4, 4, 4, 2, 2)
STARTS = (0, 4, 8, 12, 14)
RISING = (True, False, True, False, False)
UNITS = (
    (0, 2), (1, 2), (2, 2), (3, 2), (4, 2), (0, 1), (1, 3), (1, 1), (0, 3), (2, 1),
    (3, 3), (3, 1), (4, 3), (2, 3), (4, 1), (0, 0), (1, 0), (2, 0), (3, 0), (4, 0),
)
FIRST = [sum(SIZES[piece] for piece, _ in UNITS[:unit]) for unit in range(len(UNITS))]
FAR, SUM, NEAR = range(3)
AHEAD = 2


def kernel(
    source, receiver, out,
    raw, turned, own, left, right, partial, inbox, across, total, total_edge, landed, landed_edge,
    raw_sem, own_sem, ship_send, ship_recv, along_send, along_recv, ring_send, ring_recv,
    over_send, over_recv, home_send, home_recv,
):
    shots, cells, times, _ = source.shape
    share = sum(SIZES)
    wide = QUAD * cells
    owners = lax.axis_size("inline")
    me, shot = lax.axis_index("inline"), lax.axis_index("shot")
    core, low, x, high = me % 2, (me // 2) % 2, shot % RINGS, shot // RINGS
    place_in_quad, z = me % QUAD, me // QUAD
    quad = z * QUAD
    core_mate = me + 1 - 2 * core
    low_mate = me + 2 - 4 * low
    above = (me + QUAD) % owners
    below = (me + owners - QUAD) % owners
    up = high * RINGS + (x + 1) % RINGS
    down = high * RINGS + (x + RINGS - 1) % RINGS
    high_mate = (1 - high) * RINGS + x
    diagonal = low_mate + 1 - 2 * core
    peers = [
        (core_mate, shot), (low_mate, shot), (diagonal, shot), (above, shot), (below, shot),
        (me, up), (me, down), (low_mate, high_mate),
    ]
    sums_here = low == core

    def place(inline, line):
        return {"inline": inline, "shot": line}

    loads = []
    for which, array in enumerate((receiver, source)):
        for tile in range(2):
            loads.append(
                pltpu.make_async_copy(
                    array.at[:, :, :, pl.ds(tile * LANES, LANES)], raw.at[which, tile], raw_sem.at[which, tile]
                )
            )
            loads[-1].start()

    barrier = pltpu.get_barrier_semaphore()
    for inline, line in peers:
        pl.semaphore_signal(barrier, inc=1, device_id=place(inline, line), device_id_type=MESH)

    def relayout(which, tile):
        loads[2 * which + tile].wait()

        def turn(i, carry):
            rows = jnp.concatenate([raw[which, tile, s, i].astype(F32) for s in range(shots)], axis=0)
            row = cells - 1 - i if which else i
            turned[pl.ds(pl.multiple_of(row * LANES, LANES), LANES), :] = rows.T
            return carry

        def gather(y, carry):
            own[which, tile * LANES + y] = turned[pl.ds(y, cells, stride=LANES), :].astype(BF16)
            return carry

        lax.fori_loop(0, cells, turn, 0, unroll=4)
        lax.fori_loop(0, LANES, gather, 0, unroll=16)

    def rows_from(unit, half, target_core):
        piece, hop = UNITS[unit]
        start = half * LANES + ((x + hop) % RINGS) * 2 * share + target_core * share + STARTS[piece]
        return pl.ds(start, SIZES[piece])

    def rows_to(unit):
        return pl.ds(FIRST[unit], SIZES[UNITS[unit][0]])

    def slot(which, unit):
        if which:
            return left.at[QUAD - 1 - place_in_quad, rows_to(unit)]
        return right.at[2 + place_in_quad, rows_to(unit)]

    def ship(which, unit, half, target, target_core, sent_as, received_as):
        return pltpu.make_async_remote_copy(
            src_ref=own.at[which, rows_from(unit, half, target_core)],
            dst_ref=slot(which, unit),
            send_sem=ship_send.at[which, sent_as, unit],
            recv_sem=ship_recv.at[which, received_as, unit],
            device_id=place(target, shot),
            device_id_type=MESH,
        )

    def to_mate(which, unit):
        return ship(which, unit, (low + high + 1 - core) % 2, core_mate, 1 - core, 0, 0)

    def to_other(which, unit, tile):
        target_core = (tile + 1 - low + high) % 2
        return ship(which, unit, tile, quad + 2 * (1 - low) + target_core, target_core, 1 + tile, 1 + core)

    def from_other(which, unit, sender):
        return ship(which, unit, 0, low_mate, core, 1, 1 + sender)

    def keep(which, unit):
        return pltpu.make_async_copy(
            own.at[which, rows_from(unit, (low + high + core) % 2, core)], slot(which, unit), own_sem.at[which, unit]
        )

    def extend(unit, upward):
        rows = rows_to(unit)
        begin, end = (4, 0) if upward else (2, 6)
        return pltpu.make_async_remote_copy(
            src_ref=right.at[pl.ds(begin, 2), rows],
            dst_ref=right.at[pl.ds(end, 2), rows],
            send_sem=along_send.at[int(upward), unit],
            recv_sem=along_recv.at[int(upward), unit],
            device_id=place(above if upward else below, shot),
            device_id_type=MESH,
        )

    def unit_rows(unit):
        return pl.ds(FIRST[unit] * wide + unit * SUBLANES, SIZES[UNITS[unit][0]] * wide + SUBLANES)

    def piece_rows(piece):
        return pl.ds(STARTS[piece] * wide + piece * SUBLANES, SIZES[piece] * wide + SUBLANES)

    def ring(kind, unit, line):
        piece, _ = UNITS[unit]
        return pltpu.make_async_remote_copy(
            src_ref=partial.at[unit_rows(unit)],
            dst_ref=inbox.at[kind, piece_rows(piece)],
            send_sem=ring_send.at[kind, piece],
            recv_sem=ring_recv.at[kind, piece],
            device_id=place(me, line),
            device_id_type=MESH,
        )

    lane = lax.broadcasted_iota(jnp.int32, (wide, LANES), 1)
    straight = lane <= lax.broadcasted_iota(jnp.int32, (wide, LANES), 0)

    def correlate(unit, kinds):
        piece, _ = UNITS[unit]
        size = SIZES[piece]
        begin, begin_in = FIRST[unit] * wide + unit * SUBLANES, STARTS[piece] * wide + piece * SUBLANES

        @pl.when(z == 0)
        def _():
            right[0:2, rows_to(unit)] = jnp.zeros((2, size, cells, LANES), BF16)

        @pl.when(z == owners // QUAD - 1)
        def _():
            right[6:8, rows_to(unit)] = jnp.zeros((2, size, cells, LANES), BF16)

        edge = jnp.zeros((wide, LANES), F32)
        for m in range(size):
            y = FIRST[unit] + m
            contract = (((1,), (1,)), ((), ()))
            rows = jnp.concatenate([left[part, y] for part in range(QUAD)], axis=0)
            columns = jnp.concatenate([right[part, y] for part in range(2 * QUAD)], axis=0)
            product = lax.dot_general(rows, columns, contract, preferred_element_type=F32)
            a = pltpu.roll(product[:, 0:LANES], 1, axis=1, stride=1, stride_axis=0)
            b = pltpu.roll(product[:, LANES:], 1, axis=1, stride=1, stride_axis=0)
            band = jnp.where(straight, a, b)
            for kind in kinds:
                band = band + inbox[kind, begin_in + m * wide : begin_in + (m + 1) * wide, :]
            partial[begin + m * wide : begin + (m + 1) * wide, :] = band
            spot = STARTS[piece] % SUBLANES + m
            edge = jnp.where(lane == spot, pltpu.roll(b, spot, axis=1) if spot else b, edge)
        edge = edge.T[0:SUBLANES]
        for kind in kinds:
            edge = edge + inbox[kind, begin_in + size * wide : begin_in + size * wide + SUBLANES, :]
        partial[begin + size * wide : begin + size * wide + SUBLANES, :] = edge

    sent = []

    def go(copy):
        copy.start()
        sent.append(copy)

    def pass_over(unit):
        piece, _ = UNITS[unit]
        return pltpu.make_async_remote_copy(
            src_ref=partial.at[unit_rows(unit)],
            dst_ref=across.at[piece_rows(piece)],
            send_sem=over_send.at[piece],
            recv_sem=over_recv.at[piece],
            device_id=place(low_mate, high_mate),
            device_id_type=MESH,
        )

    def collect(which, unit):
        keep(which, unit).wait()
        to_mate(which, unit).wait_recv()
        for sender in range(2):
            from_other(which, unit, sender).wait_recv()

    def process(unit):
        collect(1, unit)
        extend(unit, True).wait_recv()
        extend(unit, False).wait_recv()
        piece, hop = UNITS[unit]
        rising = RISING[piece]
        toward = up if rising else down
        if hop == 2:
            correlate(unit, ())
            go(ring(FAR, unit, toward))
        elif hop == 0:
            ring(SUM, unit, toward).wait_recv()
            ring(NEAR, unit, toward).wait_recv()
            correlate(unit, (SUM, NEAR))

            @pl.when(jnp.logical_not(sums_here))
            def _():
                pass_over(unit).start()
        elif (hop == 1) == rising:
            ring(FAR, unit, toward).wait_recv()
            correlate(unit, (FAR,))
            go(ring(SUM, unit, toward))
        else:
            correlate(unit, ())
            go(ring(NEAR, unit, down if rising else up))

    def bring_home(piece, owner):
        rows = pl.ds(STARTS[piece], SIZES[piece])
        return pltpu.make_async_remote_copy(
            src_ref=total.at[rows, pl.ds((QUAD - 1 - owner) * cells, cells)],
            dst_ref=landed.at[core, rows],
            send_sem=home_send.at[owner, piece],
            recv_sem=home_recv.at[core, piece],
            device_id=place(quad + owner, shot),
            device_id_type=MESH,
        )

    def bring_edge(owner):
        return pltpu.make_async_remote_copy(
            src_ref=total_edge,
            dst_ref=landed_edge.at[core],
            send_sem=home_send.at[owner, len(SIZES)],
            recv_sem=home_recv.at[core, len(SIZES)],
            device_id=place(quad + owner, shot),
            device_id_type=MESH,
        )

    def finish(piece):
        unit = UNITS.index((piece, 0))
        size = SIZES[piece]
        begin, begin_in = FIRST[unit] * wide + unit * SUBLANES, STARTS[piece] * wide + piece * SUBLANES

        @pl.when(sums_here)
        def _():
            pass_over(unit).wait_recv()
            for m in range(size):
                total[STARTS[piece] + m] = (
                    partial[begin + m * wide : begin + (m + 1) * wide, :]
                    + across[begin_in + m * wide : begin_in + (m + 1) * wide, :]
                )
            edge = (
                partial[begin + size * wide : begin + size * wide + SUBLANES, :]
                + across[begin_in + size * wide : begin_in + size * wide + SUBLANES, :]
            )
            total_edge[piece] = edge
            for owner in (2, 3, 0, 1):

                @pl.when(place_in_quad != owner)
                def _(owner=owner):
                    bring_home(piece, owner).start()
                    if piece == len(SIZES) - 1:
                        bring_edge(owner).start()

                @pl.when(place_in_quad == owner)
                def _(owner=owner):
                    rows = slice(STARTS[piece], STARTS[piece] + size)
                    cut = slice((QUAD - 1 - owner) * cells, (QUAD - owner) * cells)
                    landed[core, rows] = total[rows, cut]
                    landed_edge[core, piece] = edge

    def forward(unit):
        collect(0, unit)
        go(extend(unit, True))
        go(extend(unit, False))

    for which in range(2):
        for tile in range(2):
            relayout(which, tile)
            if which == 0 and tile == 0:
                pl.semaphore_wait(barrier, len(peers))
            for unit in range(AHEAD):
                go(to_other(which, unit, tile))
        for unit in range(AHEAD):
            go(to_mate(which, unit))
            keep(which, unit).start()
    for unit in range(AHEAD, len(UNITS)):
        for which in range(2):
            for tile in range(2):
                go(to_other(which, unit, tile))
    for unit in range(AHEAD, len(UNITS)):
        for which in range(2):
            go(to_mate(which, unit))
            keep(which, unit).start()

    forward(0)
    for unit in range(len(UNITS)):
        if unit + 1 < len(UNITS):
            forward(unit + 1)
        if UNITS[unit] == (2, 0):
            finish(0)
        if UNITS[unit] == (4, 0):
            finish(1)
        process(unit)
    for piece in range(2, len(SIZES)):
        finish(piece)

    groups = ((0, 1), (2, 3, 4))
    for summer in range(2):
        for group, pieces in enumerate(groups):
            elsewhere = place_in_quad != (QUAD - 1) * summer

            @pl.when(elsewhere)
            def _(summer=summer, pieces=pieces):
                for piece in pieces:
                    pltpu.make_async_remote_copy(
                        src_ref=total.at[pl.ds(STARTS[piece], SIZES[piece]), pl.ds(0, cells)],
                        dst_ref=landed.at[summer, pl.ds(STARTS[piece], SIZES[piece])],
                        send_sem=home_send.at[0, piece],
                        recv_sem=home_recv.at[summer, piece],
                        device_id=place(low_mate, shot),
                        device_id_type=MESH,
                    ).wait_recv()

            rows = pl.ds(summer * share + group * SUBLANES, SUBLANES)
            for i in range(cells):
                out[i, rows, 0:LANES] = landed[
                    summer, group * SUBLANES : (group + 1) * SUBLANES, cells - 1 - i, :
                ]
    for summer in range(2):

        @pl.when(place_in_quad != (QUAD - 1) * summer)
        def _(summer=summer):
            pltpu.make_async_remote_copy(
                src_ref=total_edge,
                dst_ref=landed_edge.at[summer],
                send_sem=home_send.at[0, len(SIZES)],
                recv_sem=home_recv.at[summer, len(SIZES)],
                device_id=place(low_mate, shot),
                device_id_type=MESH,
            ).wait_recv()

        for group, pieces in enumerate(groups):
            edge = sum(landed_edge[summer, piece] for piece in pieces)
            edge = pltpu.roll(edge, (place_in_quad + 1) * cells, axis=1)
            rows = pl.ds(summer * share + group * SUBLANES, SUBLANES)
            for i in range(cells):
                back = cells - 1 - i
                out[i, rows, LANES : LANES + 1] = edge[:, back : back + 1]

    for copy in sent:
        copy.wait_send()

    @pl.when(jnp.logical_not(sums_here))
    def _():
        for piece in range(len(SIZES)):
            pass_over(UNITS.index((piece, 0))).wait_send()

    @pl.when(sums_here)
    def _():
        for owner in range(QUAD):

            @pl.when(place_in_quad != owner)
            def _(owner=owner):
                for piece in range(len(SIZES)):
                    bring_home(piece, owner).wait_send()
                bring_edge(owner).wait_send()


def on_device(source, receiver):
    shots, cells, times, cross = source.shape
    all_shots = shots * lax.axis_size("shot")
    block = cross // 8
    share = sum(SIZES)
    wide = QUAD * cells
    scale = 1.0 / (times * all_shots) ** 0.5
    lags = wide + 1
    units, pieces = len(UNITS), len(SIZES)
    image = pl.pallas_call(
        kernel,
        out_shape=jax.ShapeDtypeStruct((cells, block, lags), F32),
        in_specs=[pl.BlockSpec(memory_space=pl.ANY)] * 2,
        out_specs=pl.BlockSpec(memory_space=pltpu.VMEM),
        scratch_shapes=[
            pltpu.VMEM((2, 2, shots, cells, times, LANES), BF16),
            pltpu.VMEM((cells * LANES, LANES), F32),
            pltpu.VMEM((2, cross, cells, LANES), BF16),
            pltpu.VMEM((QUAD, 4 * share, cells, LANES), BF16),
            pltpu.VMEM((2 * QUAD, 4 * share, cells, LANES), BF16),
            pltpu.VMEM((4 * share * wide + units * SUBLANES, LANES), F32),
            pltpu.VMEM((3, share * wide + pieces * SUBLANES, LANES), F32),
            pltpu.VMEM((share * wide + pieces * SUBLANES, LANES), F32),
            pltpu.VMEM((share, wide, LANES), F32),
            pltpu.VMEM((pieces, SUBLANES, LANES), F32),
            pltpu.VMEM((2, share, cells, LANES), F32),
            pltpu.VMEM((2, pieces, SUBLANES, LANES), F32),
            pltpu.SemaphoreType.DMA((2, 2)),
            pltpu.SemaphoreType.DMA((2, units)),
            pltpu.SemaphoreType.DMA((2, 3, units)),
            pltpu.SemaphoreType.DMA((2, 3, units)),
            pltpu.SemaphoreType.DMA((2, units)),
            pltpu.SemaphoreType.DMA((2, units)),
            pltpu.SemaphoreType.DMA((3, pieces)),
            pltpu.SemaphoreType.DMA((3, pieces)),
            pltpu.SemaphoreType.DMA((pieces,)),
            pltpu.SemaphoreType.DMA((pieces,)),
            pltpu.SemaphoreType.DMA((QUAD, pieces + 1)),
            pltpu.SemaphoreType.DMA((2, pieces + 1)),
        ],
        compiler_params=pltpu.CompilerParams(collective_id=0, has_side_effects=True, vmem_limit_bytes=60 * 2**20),
    )(source, receiver)
    return jnp.transpose(image * scale, (2, 0, 1))


def solution(mesh):
    placed = (P("shot", "inline", None, None), P("shot", "inline", None, None))
    return jax.shard_map(
        on_device, mesh=mesh, in_specs=placed, out_specs=P(None, "inline", "shot"), check_vma=False
    )
```

time: 418 us -> 79.7 us (0.19)
  waiting for transfers between devices: 207 us -> 0 us
  local copies, waits for them, and re-layouts: 167 us -> 0 us
  Pallas kernels: 0 us -> 76.6 us
  matrix products: 14.3 us -> 0 us
  between operations: 13.4 us -> 0.01 us
  starting transfers between devices: 12.4 us -> 0 us
    reduce_scatter x1 -> x0, waiting for transfers between devices: 122 us -> none  [on_device(): lax.psum_scatter(partial_image, 'shot', scatter_dimension=2, tiled=True)]
    ppermute x4 -> x0, waiting for transfers between devices: 85 us -> none  [shifted(): lax.ppermute(value, axis, [(source, source + steps) for source in range(i...]
    pallas_call x0 -> x1, Pallas kernels: none -> 76.6 us  [on_device(): pl.pallas_call(kernel, out_shape=jax.ShapeDtypeStruct((cells, block, lags...]
    ppermute x4 -> x0, local copies, waits for them, and re-layouts: 60.9 us -> none  [shifted(): lax.ppermute(value, axis, [(source, source + steps) for source in range(i...]
    concatenate x1 -> x0, local copies, waits for them, and re-layouts: 44.4 us -> none  [extend(): jnp.concatenate((far_left, near_left, receiver, near_right, far_right), a...]
    unnamed x4 -> x0, local copies, waits for them, and re-layouts: 27.2 us -> none
    transpose x3 -> x0, local copies, waits for them, and re-layouts: 22.5 us -> none  [the longest x2 13.4 us: band_rows(): return jnp.transpose(skewed, (1, 0, 2))]
    dot_general x1 -> x0, matrix products: 14.3 us -> none  [correlate(): jnp.einsum('sity,szty->izy', source, extended, preferred_element_type=jnp...]
  transfers between devices with their start and end apart: 5 -> 0, of which waited for: 3 -> 0; matrix products, arithmetic and copies ran while one was open for 18% -> 0% of each run, Pallas kernels for 0% -> 0%
where the time goes in v2:
time: 79.7 us; the launch traced here: 78.9 us
  Pallas kernels  76.6 us (96%)
  other arithmetic  2.31 us (3%)
    pallas_call x1, Pallas kernels, on_device(): pl.pallas_call(kernel, out_shape=jax.ShapeDtypeStruct((cells, block, lags...  76.6 us
    transpose x1, other arithmetic, on_device(): return jnp.transpose(image * scale, (2, 0, 1))  2.31 us

profile of v2, /device:TPU:1, one launch (start us, length us, event | category | flops | bytes accessed | tf_op | source)
XLA Modules:
  0.0 78.9 jit_solution(12705388819224939957)
XLA Ops:
  0.0 76.6 %shard_map.28 = f32[32,32,129]{2,1,0:T(8,128)} custom-call(bf16[4,32,32,256]{3,2,1,0:T(8,128)(2,1)} %source.1, bf16[4,32,32,256]{3,2,1,0:T(8,128)(2,1)} %receiver.1), custom_call_target="tpu_custom_call" | custom-call | tf_op jit(solution)/shard_map/pallas_call | solution.py:401
  76.6 2.3 %multiply_bitcast_fusion = f32[129,32,32]{0,2,1:T(8,128)} fusion(f32[32,32,129]{2,1,0:T(8,128)} %shard_map.28), kind=kLoop, calls=%fused_computation | loop fusion | flops 132096 | bytes 1056768 | tf_op jit(solution)/shard_map/transpose | solution.py:434

commit v3 on v2

v3 whole, which is shorter than its diff:
```python
import functools

import jax
import jax.numpy as jnp
from jax import lax
from jax.experimental import pallas as pl
from jax.experimental.pallas import tpu as pltpu
from jax.sharding import PartitionSpec as P

MESH = pl.DeviceIdType.MESH
F32 = jnp.float32
BF16 = jnp.bfloat16
LANES = 128
SUBLANES = 8
RINGS = 4
QUAD = 4
SIZES = (4, 4, 4, 2, 2)
STARTS = (0, 4, 8, 12, 14)
RISING = (True, False, True, False, False)
UNITS = (
    (0, 2), (1, 2), (2, 2), (3, 2), (4, 2), (0, 1), (1, 3), (1, 1), (0, 3), (2, 1),
    (2, 3), (3, 3), (3, 1), (0, 0), (4, 3), (4, 1), (1, 0), (2, 0), (3, 0), (4, 0),
)
GROUPS = ((0, 2), (2, 5))
FIRST = [sum(SIZES[piece] for piece, _ in UNITS[:unit]) for unit in range(len(UNITS))]
FAR, SUM, NEAR = range(3)
AHEAD = 2
LEAD = 3
SPLIT = len(UNITS) - 3


def kernel(
    scale, source, receiver, out,
    raw, turned, own, held, beside, partial, inbox, across, total, total_edge, landed, landed_edge,
    raw_sem, own_sem, ship_send, ship_recv, along_send, along_recv, ring_send, ring_recv,
    over_send, over_recv, home_send, home_recv,
):
    shots, cells, times, _ = source.shape
    share = sum(SIZES)
    wide = QUAD * cells
    owners = lax.axis_size("inline")
    me, shot = lax.axis_index("inline"), lax.axis_index("shot")
    core, low, x, high = me % 2, (me // 2) % 2, shot % RINGS, shot // RINGS
    place_in_quad, z = me % QUAD, me // QUAD
    quad = z * QUAD
    core_mate = me + 1 - 2 * core
    low_mate = me + 2 - 4 * low
    above = (me + QUAD) % owners
    below = (me + owners - QUAD) % owners
    up = high * RINGS + (x + 1) % RINGS
    down = high * RINGS + (x + RINGS - 1) % RINGS
    high_mate = (1 - high) * RINGS + x
    diagonal = low_mate + 1 - 2 * core
    peers = [
        (core_mate, shot), (low_mate, shot), (diagonal, shot), (above, shot), (below, shot),
        (me, up), (me, down), (low_mate, high_mate),
    ]
    sums_here = low == core

    def place(inline, line):
        return {"inline": inline, "shot": line}

    loads = []
    tiles = [pl.multiple_of(((high + 1 + role) % 2) * LANES, LANES) for role in range(2)]
    for tile in range(2):
        for which, array in enumerate((receiver, source)):
            loads.append(
                pltpu.make_async_copy(
                    array.at[:, :, :, pl.ds(tiles[tile], LANES)], raw.at[which, tile], raw_sem.at[which, tile]
                )
            )
            loads[-1].start()

    barrier = pltpu.get_barrier_semaphore()
    for inline, line in peers:
        pl.semaphore_signal(barrier, inc=1, device_id=place(inline, line), device_id_type=MESH)

    def relayout(which, tile):
        loads[2 * tile + which].wait()

        def turn(i, carry):
            rows = jnp.concatenate([raw[which, tile, s, i] for s in range(shots)], axis=0)
            row = cells - 1 - i if which else i
            turned[pl.ds(pl.multiple_of(row * LANES, LANES), LANES), :] = rows.T.astype(F32)
            return carry

        def gather(y, carry):
            own[tiles[tile] + y, which * cells : (which + 1) * cells] = turned[pl.ds(y, cells, stride=LANES), :].astype(BF16)
            return carry

        lax.fori_loop(0, cells, turn, 0, unroll=8)
        lax.fori_loop(0, LANES, gather, 0, unroll=16)

    def rows_from(unit, half, target_core):
        piece, hop = UNITS[unit]
        start = half * LANES + ((x + hop) % RINGS) * 2 * share + target_core * share + STARTS[piece]
        return pl.ds(start, SIZES[piece])

    def rows_to(unit):
        return pl.ds(FIRST[unit], SIZES[UNITS[unit][0]])

    def ship(unit, half, target, target_core, sent_as, received_as, part=None):
        inner = pl.ds(0, 2 * cells) if part is None else pl.ds(part * cells, cells)
        column = len(UNITS) + unit - SPLIT if part else unit
        return pltpu.make_async_remote_copy(
            src_ref=own.at[rows_from(unit, half, target_core), inner],
            dst_ref=held.at[place_in_quad, rows_to(unit), inner],
            send_sem=ship_send.at[sent_as, column],
            recv_sem=ship_recv.at[received_as, column],
            device_id=place(target, shot),
            device_id_type=MESH,
        )

    def to_mate(unit):
        return ship(unit, (low + high + 1 - core) % 2, core_mate, 1 - core, 0, 0)

    def to_other(unit, role, part=None):
        target_core = (role - low) % 2
        target = quad + 2 * (1 - low) + target_core
        return ship(unit, (high + 1 + role) % 2, target, target_core, 1 + role, 1 + core, part)

    def from_other(unit, part=None):
        for sender in range(2):
            ship(unit, 0, low_mate, core, 1, 1 + sender, part).wait_recv()

    def keep(unit):
        return pltpu.make_async_copy(
            own.at[rows_from(unit, (low + high + core) % 2, core)],
            held.at[place_in_quad, rows_to(unit)],
            own_sem.at[unit],
        )

    def extend(unit, upward):
        rows = rows_to(unit)
        begin, end = (2, 0) if upward else (0, 2)
        return pltpu.make_async_remote_copy(
            src_ref=held.at[pl.ds(begin, 2), rows, pl.ds(0, cells)],
            dst_ref=beside.at[pl.ds(end, 2), rows],
            send_sem=along_send.at[int(upward), unit],
            recv_sem=along_recv.at[int(upward), unit],
            device_id=place(above if upward else below, shot),
            device_id_type=MESH,
        )

    def unit_rows(unit):
        return pl.ds(FIRST[unit] * wide + unit * SUBLANES, SIZES[UNITS[unit][0]] * wide + SUBLANES)

    def piece_rows(piece):
        return pl.ds(STARTS[piece] * wide + piece * SUBLANES, SIZES[piece] * wide + SUBLANES)

    def ring(kind, unit, line):
        piece, _ = UNITS[unit]
        return pltpu.make_async_remote_copy(
            src_ref=partial.at[unit_rows(unit)],
            dst_ref=inbox.at[kind, piece_rows(piece)],
            send_sem=ring_send.at[kind, piece],
            recv_sem=ring_recv.at[kind, piece],
            device_id=place(me, line),
            device_id_type=MESH,
        )

    lane = lax.broadcasted_iota(jnp.int32, (wide, LANES), 1)
    straight = lane <= lax.broadcasted_iota(jnp.int32, (wide, LANES), 0)

    def correlate(unit, kinds):
        piece, _ = UNITS[unit]
        size = SIZES[piece]
        begin, begin_in = FIRST[unit] * wide + unit * SUBLANES, STARTS[piece] * wide + piece * SUBLANES

        @pl.when(z == 0)
        def _():
            beside[0:2, rows_to(unit)] = jnp.zeros((2, size, cells, LANES), BF16)

        @pl.when(z == owners // QUAD - 1)
        def _():
            beside[2:4, rows_to(unit)] = jnp.zeros((2, size, cells, LANES), BF16)

        edge = jnp.zeros((wide, LANES), F32)
        for m in range(size):
            y = FIRST[unit] + m
            contract = (((1,), (1,)), ((), ()))
            rows = jnp.concatenate([held[QUAD - 1 - part, y, cells:] for part in range(QUAD)], axis=0)
            columns = [beside[0, y], beside[1, y]] + [held[part, y, :cells] for part in range(QUAD)]
            columns = jnp.concatenate(columns + [beside[2, y], beside[3, y]], axis=0)
            product = lax.dot_general(rows, columns, contract, preferred_element_type=F32)
            a = pltpu.roll(product[:, 0:LANES], 1, axis=1, stride=1, stride_axis=0)
            b = pltpu.roll(product[:, LANES:], 1, axis=1, stride=1, stride_axis=0)
            band = jnp.where(straight, a, b)
            for kind in kinds:
                band = band + inbox[kind, begin_in + m * wide : begin_in + (m + 1) * wide, :]
            partial[begin + m * wide : begin + (m + 1) * wide, :] = band
            spot = STARTS[piece] % SUBLANES + m
            edge = jnp.where(lane == spot, pltpu.roll(b, spot, axis=1) if spot else b, edge)
        edge = edge.T[0:SUBLANES]
        for kind in kinds:
            edge = edge + inbox[kind, begin_in + size * wide : begin_in + size * wide + SUBLANES, :]
        partial[begin + size * wide : begin + size * wide + SUBLANES, :] = edge

    sent = []

    def go(copy):
        copy.start()
        sent.append(copy)

    def pass_over(unit):
        piece, _ = UNITS[unit]
        return pltpu.make_async_remote_copy(
            src_ref=partial.at[unit_rows(unit)],
            dst_ref=across.at[piece_rows(piece)],
            send_sem=over_send.at[piece],
            recv_sem=over_recv.at[piece],
            device_id=place(low_mate, high_mate),
            device_id_type=MESH,
        )

    def process(unit):
        if unit >= SPLIT:
            from_other(unit, 1)
        extend(unit, True).wait_recv()
        extend(unit, False).wait_recv()
        piece, hop = UNITS[unit]
        rising = RISING[piece]
        toward = up if rising else down
        if hop == 2:
            correlate(unit, ())
            go(ring(FAR, unit, toward))
        elif hop == 0:
            ring(SUM, unit, toward).wait_recv()
            ring(NEAR, unit, toward).wait_recv()
            correlate(unit, (SUM, NEAR))

            @pl.when(jnp.logical_not(sums_here))
            def _():
                pass_over(unit).start()
        elif (hop == 1) == rising:
            ring(FAR, unit, toward).wait_recv()
            correlate(unit, (FAR,))
            go(ring(SUM, unit, toward))
        else:
            correlate(unit, ())
            go(ring(NEAR, unit, down if rising else up))

    def bring_home(piece, owner):
        rows = pl.ds(STARTS[piece], SIZES[piece])
        return pltpu.make_async_remote_copy(
            src_ref=total.at[rows, pl.ds((QUAD - 1 - owner) * cells, cells)],
            dst_ref=landed.at[core, rows],
            send_sem=home_send.at[owner, piece],
            recv_sem=home_recv.at[core, piece],
            device_id=place(quad + owner, shot),
            device_id_type=MESH,
        )

    def bring_edge(group, owner):
        rows = pl.ds(GROUPS[group][0], GROUPS[group][1] - GROUPS[group][0])
        return pltpu.make_async_remote_copy(
            src_ref=total_edge.at[rows],
            dst_ref=landed_edge.at[core, rows],
            send_sem=home_send.at[owner, len(SIZES) + group],
            recv_sem=home_recv.at[core, len(SIZES) + group],
            device_id=place(quad + owner, shot),
            device_id_type=MESH,
        )

    def finish(piece):
        unit = UNITS.index((piece, 0))
        size = SIZES[piece]
        begin, begin_in = FIRST[unit] * wide + unit * SUBLANES, STARTS[piece] * wide + piece * SUBLANES

        @pl.when(sums_here)
        def _():
            pass_over(unit).wait_recv()
            for m in range(size):
                total[STARTS[piece] + m] = (
                    partial[begin + m * wide : begin + (m + 1) * wide, :]
                    + across[begin_in + m * wide : begin_in + (m + 1) * wide, :]
                )
            edge = (
                partial[begin + size * wide : begin + size * wide + SUBLANES, :]
                + across[begin_in + size * wide : begin_in + size * wide + SUBLANES, :]
            )
            total_edge[piece] = edge
            for owner in (2, 3, 0, 1):

                @pl.when(place_in_quad != owner)
                def _(owner=owner):
                    bring_home(piece, owner).start()
                    for group, (_, stop) in enumerate(GROUPS):
                        if piece == stop - 1:
                            bring_edge(group, owner).start()

                @pl.when(place_in_quad == owner)
                def _(owner=owner):
                    rows = slice(STARTS[piece], STARTS[piece] + size)
                    cut = slice((QUAD - 1 - owner) * cells, (QUAD - owner) * cells)
                    landed[core, rows] = total[rows, cut]
                    landed_edge[core, piece] = edge

    def forward(unit):
        keep(unit).wait()
        to_mate(unit).wait_recv()
        from_other(unit, 0 if unit >= SPLIT else None)
        go(extend(unit, True))
        go(extend(unit, False))

    def land(group):
        pieces = range(*GROUPS[group])
        for summer in range(2):

            @pl.when(place_in_quad != (QUAD - 1) * summer)
            def _(summer=summer):
                for piece in pieces:
                    rows = pl.ds(STARTS[piece], SIZES[piece])
                    pltpu.make_async_remote_copy(
                        src_ref=total.at[rows, pl.ds(0, cells)],
                        dst_ref=landed.at[summer, rows],
                        send_sem=home_send.at[0, piece],
                        recv_sem=home_recv.at[summer, piece],
                        device_id=place(low_mate, shot),
                        device_id_type=MESH,
                    ).wait_recv()
                rows = pl.ds(GROUPS[group][0], GROUPS[group][1] - GROUPS[group][0])
                pltpu.make_async_remote_copy(
                    src_ref=total_edge.at[rows],
                    dst_ref=landed_edge.at[summer, rows],
                    send_sem=home_send.at[0, len(SIZES) + group],
                    recv_sem=home_recv.at[summer, len(SIZES) + group],
                    device_id=place(low_mate, shot),
                    device_id_type=MESH,
                ).wait_recv()

            edge = sum(landed_edge[summer, piece] for piece in pieces) * scale
            edge = pltpu.roll(edge, (place_in_quad + 1) * cells, axis=1)
            rows = pl.ds(summer * share + group * SUBLANES, SUBLANES)
            for i in range(cells):
                back = cells - 1 - i
                strip = landed[summer, group * SUBLANES : (group + 1) * SUBLANES, back, :]
                out[i, rows, 0:LANES] = strip * scale
                out[i, rows, LANES : LANES + 1] = edge[:, back : back + 1]

    queue = [[(unit, role, None) for unit in range(SPLIT)] for role in range(2)]
    for role in range(2):
        for part in range(2):
            queue[role] += [(unit, role, part) for unit in range(SPLIT, len(UNITS))]
    relayout(0, 0)
    relayout(1, 0)
    pl.semaphore_wait(barrier, len(peers))
    for item in queue[0][:LEAD]:
        go(to_other(*item))
    relayout(0, 1)
    relayout(1, 1)
    for unit in range(AHEAD):
        go(to_mate(unit))
        keep(unit).start()
    for index in range(len(queue[0]) + LEAD):
        if index >= LEAD:
            go(to_other(*queue[1][index - LEAD]))
        if LEAD <= index < len(queue[0]):
            go(to_other(*queue[0][index]))
        if AHEAD <= index - LEAD + AHEAD < len(UNITS):
            go(to_mate(index - LEAD + AHEAD))
            keep(index - LEAD + AHEAD).start()

    forward(0)
    for unit in range(len(UNITS)):
        if unit + 1 < SPLIT:
            forward(unit + 1)
        if UNITS[unit] == (1, 0):
            finish(0)
        if UNITS[unit] == (4, 0):
            finish(1)
        process(unit)
        if unit + 1 == SPLIT:
            for later in range(SPLIT, len(UNITS)):
                forward(later)
    finish(2)
    land(0)
    finish(3)
    finish(4)
    land(1)

    for copy in sent:
        copy.wait_send()

    @pl.when(jnp.logical_not(sums_here))
    def _():
        for piece in range(len(SIZES)):
            pass_over(UNITS.index((piece, 0))).wait_send()

    @pl.when(sums_here)
    def _():
        for owner in range(QUAD):

            @pl.when(place_in_quad != owner)
            def _(owner=owner):
                for piece in range(len(SIZES)):
                    bring_home(piece, owner).wait_send()
                for group in range(len(GROUPS)):
                    bring_edge(group, owner).wait_send()


def on_device(source, receiver):
    shots, cells, times, cross = source.shape
    all_shots = shots * lax.axis_size("shot")
    block = cross // 8
    share = sum(SIZES)
    wide = QUAD * cells
    scale = 1.0 / (times * all_shots) ** 0.5
    lags = wide + 1
    units, pieces = len(UNITS), len(SIZES)
    image = pl.pallas_call(
        functools.partial(kernel, scale),
        out_shape=jax.ShapeDtypeStruct((cells, block, lags), F32),
        in_specs=[pl.BlockSpec(memory_space=pl.ANY)] * 2,
        out_specs=pl.BlockSpec(memory_space=pltpu.VMEM),
        scratch_shapes=[
            pltpu.VMEM((2, 2, shots, cells, times, LANES), BF16),
            pltpu.VMEM((cells * LANES, LANES), F32),
            pltpu.VMEM((cross, 2 * cells, LANES), BF16),
            pltpu.VMEM((QUAD, 4 * share, 2 * cells, LANES), BF16),
            pltpu.VMEM((QUAD, 4 * share, cells, LANES), BF16),
            pltpu.VMEM((4 * share * wide + units * SUBLANES, LANES), F32),
            pltpu.VMEM((3, share * wide + pieces * SUBLANES, LANES), F32),
            pltpu.VMEM((share * wide + pieces * SUBLANES, LANES), F32),
            pltpu.VMEM((share, wide, LANES), F32),
            pltpu.VMEM((pieces, SUBLANES, LANES), F32),
            pltpu.VMEM((2, share, cells, LANES), F32),
            pltpu.VMEM((2, pieces, SUBLANES, LANES), F32),
            pltpu.SemaphoreType.DMA((2, 2)),
            pltpu.SemaphoreType.DMA((units,)),
            pltpu.SemaphoreType.DMA((3, 2 * units - SPLIT)),
            pltpu.SemaphoreType.DMA((3, 2 * units - SPLIT)),
            pltpu.SemaphoreType.DMA((2, units)),
            pltpu.SemaphoreType.DMA((2, units)),
            pltpu.SemaphoreType.DMA((3, pieces)),
            pltpu.SemaphoreType.DMA((3, pieces)),
            pltpu.SemaphoreType.DMA((pieces,)),
            pltpu.SemaphoreType.DMA((pieces,)),
            pltpu.SemaphoreType.DMA((QUAD, pieces + len(GROUPS))),
            pltpu.SemaphoreType.DMA((2, pieces + len(GROUPS))),
        ],
        compiler_params=pltpu.CompilerParams(collective_id=0, has_side_effects=True, vmem_limit_bytes=60 * 2**20),
    )(source, receiver)
    return jnp.transpose(image, (2, 0, 1))


def solution(mesh):
    placed = (P("shot", "inline", None, None), P("shot", "inline", None, None))
    return jax.shard_map(
        on_device, mesh=mesh, in_specs=placed, out_specs=P(None, "inline", "shot"), check_vma=False
    )
```

time: 79.7 us -> 78.6 us (0.986)
  other arithmetic: 2.31 us -> 0 us
  local copies, waits for them, and re-layouts: 0 us -> 2.31 us
    transpose x1 -> x0, other arithmetic: 2.31 us -> none  [on_device(): return jnp.transpose(image * scale, (2, 0, 1))]
    unnamed x0 -> x1, local copies, waits for them, and re-layouts: none -> 2.31 us
where the time goes in v3:
time: 78.6 us; the launch traced here: 78.5 us
  Pallas kernels  76.2 us (97%)
  local copies, waits for them, and re-layouts  2.31 us (3%)
    pallas_call x1, Pallas kernels, on_device(): pl.pallas_call(functools.partial(kernel, scale), out_shape=jax.ShapeDtype...  76.2 us
    unnamed x1, local copies, waits for them, and re-layouts  2.31 us

profile of v3, /device:TPU:1, one launch (start us, length us, event | category | flops | bytes accessed | tf_op | source)
XLA Modules:
  0.0 78.5 jit_solution(17254645899511696797)
XLA Ops:
  0.0 76.2 %shard_map.28 = f32[32,32,129]{2,1,0:T(8,128)} custom-call(bf16[4,32,32,256]{3,2,1,0:T(8,128)(2,1)} %source.1, bf16[4,32,32,256]{3,2,1,0:T(8,128)(2,1)} %receiver.1), custom_call_target="tpu_custom_call" | custom-call | tf_op jit(solution)/shard_map/pallas_call | solution.py:411
  76.2 2.3 %copy.4 = f32[129,32,32]{0,2,1:T(8,128)} copy(f32[129,32,32]{0,2,1:T(8,128)} %bitcast.1) | data formatting | bytes 1056768

commit v4 on v3

--- a/solution.py
+++ b/solution.py
@@ -52,9 +52,9 @@
     high_mate = (1 - high) * RINGS + x
     diagonal = low_mate + 1 - 2 * core
     peers = [
-        (core_mate, shot), (low_mate, shot), (diagonal, shot), (above, shot), (below, shot),
-        (me, up), (me, down), (low_mate, high_mate),
+        (core_mate, shot), (low_mate, shot), (diagonal, shot), (me, up), (me, down), (low_mate, high_mate),
     ]
+    last = owners // QUAD - 1
     sums_here = low == core
 
     def place(inline, line):
@@ -74,6 +74,11 @@
     barrier = pltpu.get_barrier_semaphore()
     for inline, line in peers:
         pl.semaphore_signal(barrier, inc=1, device_id=place(inline, line), device_id_type=MESH)
+    for there, inline in ((z < last, above), (z > 0, below)):
+
+        @pl.when(there)
+        def _(inline=inline):
+            pl.semaphore_signal(barrier, inc=1, device_id=place(inline, shot), device_id_type=MESH)
 
     def relayout(which, tile):
         loads[2 * tile + which].wait()
@@ -166,14 +171,6 @@
         piece, _ = UNITS[unit]
         size = SIZES[piece]
         begin, begin_in = FIRST[unit] * wide + unit * SUBLANES, STARTS[piece] * wide + piece * SUBLANES
-
-        @pl.when(z == 0)
-        def _():
-            beside[0:2, rows_to(unit)] = jnp.zeros((2, size, cells, LANES), BF16)
-
-        @pl.when(z == owners // QUAD - 1)
-        def _():
-            beside[2:4, rows_to(unit)] = jnp.zeros((2, size, cells, LANES), BF16)
 
         edge = jnp.zeros((wide, LANES), F32)
         for m in range(size):
@@ -216,8 +213,15 @@
     def process(unit):
         if unit >= SPLIT:
             from_other(unit, 1)
-        extend(unit, True).wait_recv()
-        extend(unit, False).wait_recv()
+
+        @pl.when(z > 0)
+        def _():
+            extend(unit, True).wait_recv()
+
+        @pl.when(z < last)
+        def _():
+            extend(unit, False).wait_recv()
+
         piece, hop = UNITS[unit]
         rising = RISING[piece]
         toward = up if rising else down
@@ -300,8 +304,15 @@
         keep(unit).wait()
         to_mate(unit).wait_recv()
         from_other(unit, 0 if unit >= SPLIT else None)
-        go(extend(unit, True))
-        go(extend(unit, False))
+
+        @pl.when(z < last)
+        def _():
+            extend(unit, True).start()
+
+        @pl.when(z > 0)
+        def _():
+            extend(unit, False).start()
+
 
     def land(group):
         pieces = range(*GROUPS[group])
@@ -344,7 +355,7 @@
             queue[role] += [(unit, role, part) for unit in range(SPLIT, len(UNITS))]
     relayout(0, 0)
     relayout(1, 0)
-    pl.semaphore_wait(barrier, len(peers))
+    pl.semaphore_wait(barrier, len(peers) + jnp.where(z < last, 1, 0) + jnp.where(z > 0, 1, 0))
     for item in queue[0][:LEAD]:
         go(to_other(*item))
     relayout(0, 1)
@@ -360,6 +371,17 @@
         if AHEAD <= index - LEAD + AHEAD < len(UNITS):
             go(to_mate(index - LEAD + AHEAD))
             keep(index - LEAD + AHEAD).start()
+
+    for missing, edge in ((z == 0, 0), (z == last, 2)):
+
+        @pl.when(missing)
+        def _(edge=edge):
+            def clear(y, carry):
+                beside[edge, y] = jnp.zeros((cells, LANES), BF16)
+                beside[edge + 1, y] = jnp.zeros((cells, LANES), BF16)
+                return carry
+
+            lax.fori_loop(0, QUAD * share, clear, 0, unroll=4)
 
     forward(0)
     for unit in range(len(UNITS)):
@@ -381,6 +403,12 @@
 
     for copy in sent:
         copy.wait_send()
+    for there, upward in ((z < last, True), (z > 0, False)):
+
+        @pl.when(there)
+        def _(upward=upward):
+            for unit in range(len(UNITS)):
+                extend(unit, upward).wait_send()
 
     @pl.when(jnp.logical_not(sums_here))
     def _():
@@ -410,7 +438,7 @@
     units, pieces = len(UNITS), len(SIZES)
     image = pl.pallas_call(
         functools.partial(kernel, scale),
-        out_shape=jax.ShapeDtypeStruct((cells, block, lags), F32),
+        out_shape=pltpu.VMEM((cells, block, lags), F32),
         in_specs=[pl.BlockSpec(memory_space=pl.ANY)] * 2,
         out_specs=pl.BlockSpec(memory_space=pltpu.VMEM),
         scratch_shapes=[

time: 78.6 us -> 74.3 us (0.945)
  Pallas kernels: 76.2 us -> 73.3 us
  local copies, waits for them, and re-layouts: 2.31 us -> 0.97 us
    pallas_call x1, Pallas kernels: 76.2 us -> 73.3 us  [on_device(): pl.pallas_call(functools.partial(kernel, scale), out_shape=pltpu.VMEM((ce...]
    unnamed x1, local copies, waits for them, and re-layouts: 2.31 us -> 0.97 us
where the time goes in v4:
time: 74.3 us; the launch traced here: 74.2 us
  Pallas kernels  73.3 us (99%)
  local copies, waits for them, and re-layouts  0.97 us (1%)
    pallas_call x1, Pallas kernels, on_device(): pl.pallas_call(functools.partial(kernel, scale), out_shape=pltpu.VMEM((ce...  73.3 us

profile of v4, /device:TPU:1, one launch (start us, length us, event | category | flops | bytes accessed | tf_op | source)
XLA Modules:
  0.0 74.2 jit_solution(11302509795641651465)
XLA Ops:
  0.0 73.3 %shard_map.28 = f32[32,32,129]{2,1,0:T(8,128)S(1)} custom-call(bf16[4,32,32,256]{3,2,1,0:T(8,128)(2,1)} %source.1, bf16[4,32,32,256]{3,2,1,0:T(8,128)(2,1)} %receiver.1), custom_call_target="tpu_custom_call" | custom-call | tf_op jit(solution)/shard_map/pallas_call | solution.py:439
  73.3 1.0 %copy.4 = f32[129,32,32]{0,2,1:T(8,128)} copy(f32[129,32,32]{0,2,1:T(8,128)S(1)} %bitcast.1) | data formatting | bytes 1056768

commit v5 on v4

--- a/solution.py
+++ b/solution.py
@@ -26,7 +26,7 @@
 FAR, SUM, NEAR = range(3)
 AHEAD = 2
 LEAD = 3
-SPLIT = len(UNITS) - 3
+SPLIT = len(UNITS) - 7
 
 
 def kernel(
@@ -384,9 +384,10 @@
             lax.fori_loop(0, QUAD * share, clear, 0, unroll=4)
 
     forward(0)
+    forward(1)
     for unit in range(len(UNITS)):
-        if unit + 1 < SPLIT:
-            forward(unit + 1)
+        if unit + 2 < SPLIT:
+            forward(unit + 2)
         if UNITS[unit] == (1, 0):
             finish(0)
         if UNITS[unit] == (4, 0):

time: 74.3 us -> 68.9 us (0.927)
  Pallas kernels: 73.3 us -> 67.8 us
    pallas_call x1, Pallas kernels: 73.3 us -> 67.8 us  [on_device(): pl.pallas_call(functools.partial(kernel, scale), out_shape=pltpu.VMEM((ce...]
where the time goes in v5:
time: 68.9 us; the launch traced here: 68.8 us
  Pallas kernels  67.8 us (98%)
  local copies, waits for them, and re-layouts  0.97 us (1%)
    pallas_call x1, Pallas kernels, on_device(): pl.pallas_call(functools.partial(kernel, scale), out_shape=pltpu.VMEM((ce...  67.8 us

profile of v5, /device:TPU:1, one launch (start us, length us, event | category | flops | bytes accessed | tf_op | source)
XLA Modules:
  0.0 68.8 jit_solution(15928039104583272071)
XLA Ops:
  0.0 67.8 %shard_map.28 = f32[32,32,129]{2,1,0:T(8,128)S(1)} custom-call(bf16[4,32,32,256]{3,2,1,0:T(8,128)(2,1)} %source.1, bf16[4,32,32,256]{3,2,1,0:T(8,128)(2,1)} %receiver.1), custom_call_target="tpu_custom_call" | custom-call | tf_op jit(solution)/shard_map/pallas_call | solution.py:440
  67.8 1.0 %copy.4 = f32[129,32,32]{0,2,1:T(8,128)} copy(f32[129,32,32]{0,2,1:T(8,128)S(1)} %bitcast.1) | data formatting | bytes 1056768

commit v6 on v5

--- a/solution.py
+++ b/solution.py
@@ -26,7 +26,7 @@
 FAR, SUM, NEAR = range(3)
 AHEAD = 2
 LEAD = 3
-SPLIT = len(UNITS) - 7
+SPLIT = len(UNITS) - 9
 
 
 def kernel(

time: 68.9 us -> 69.1 us (level)
  no operation moved by 1% of the time
where the time goes in v6:
time: 69.1 us; the launch traced here: 68.9 us
  Pallas kernels  67.9 us (98%)
  local copies, waits for them, and re-layouts  0.97 us (1%)
    pallas_call x1, Pallas kernels, on_device(): pl.pallas_call(functools.partial(kernel, scale), out_shape=pltpu.VMEM((ce...  67.9 us

profile of v6, /device:TPU:1, one launch (start us, length us, event | category | flops | bytes accessed | tf_op | source)
XLA Modules:
  0.0 68.9 jit_solution(10669939791122600420)
XLA Ops:
  0.0 67.9 %shard_map.28 = f32[32,32,129]{2,1,0:T(8,128)S(1)} custom-call(bf16[4,32,32,256]{3,2,1,0:T(8,128)(2,1)} %source.1, bf16[4,32,32,256]{3,2,1,0:T(8,128)(2,1)} %receiver.1), custom_call_target="tpu_custom_call" | custom-call | tf_op jit(solution)/shard_map/pallas_call | solution.py:440
  67.9 1.0 %copy.4 = f32[129,32,32]{0,2,1:T(8,128)} copy(f32[129,32,32]{0,2,1:T(8,128)S(1)} %bitcast.1) | data formatting | bytes 1056768
